TPU v7x, 256 devices: a whole 4x4x8 slice. The times are simulated.
256 devices in a mesh: tm: 8 (over z_lo, core), chan: 32 (over z_hi, y, x).
Axes of the slice: x: 4, y: 4, z: 8 (z_hi: 2, z_lo: 4; z = z_hi * 4 + z_lo), core: 2. Of those that a mesh axis runs over, the one named last changes fastest.
Arguments:
- raw_strain: bfloat16 [256000, 4096], P('tm', 'chan'), may hold values from -600 to 600
- source_blocks: int32 [2], replicated, may hold values from 0 to 27, as said below
- band_bins: int32 [2], replicated, may hold values from 0 to 20, as said below
Outputs:
- cross_spectra: bfloat16 [1280, 2, 20, 4096], P('tm', None, None, 'chan')
Inputs may be any that keep to these rules, and one draw needn't show every extreme that they name: `source_blocks`: each entry is the index of the channel block of 128 channels at which a virtual-source block of 640 channels begins; the two entries differ, one of them is always the last possible start, and the blocks may intersect. band_bins[0] is at most 2 and band_bins[1] is at least 18.
All inputs are finite; a program needn't handle non-finite values.
Results may differ from a plain program's by a relative error of at most 0.0091.
Values may be sent and summed in bfloat16 or wider, within the bound.
A program may use at most 64 MiB of HBM per device.

v0:
```python
import math
import jax
import jax.numpy as jnp
import numpy as np
from jax import lax
from jax.sharding import PartitionSpec as P

NW = 16
WIN = 500
NB = 20
VS = 640
TAPS = 64
DECIM = 4


def from_behind(value, axis, steps):
    count = lax.axis_size(axis)
    initial, last = (max(0, -steps), min(count, count - steps))
    return lax.ppermute(value, axis, [(source, source + steps) for source in range(initial, last)])


def carried_in(part, axis, combine, identity):
    place = lax.axis_index(axis)
    gathered = jax.tree.map(lambda a: lax.all_gather(a, axis), part)
    state = jax.tree.map(lambda a, e: jnp.zeros_like(a) + jnp.asarray(e, a.dtype), part, identity)

    def one(step, state):
        return combine(
            state, jax.tree.map(lambda a: lax.dynamic_index_in_dim(a, step, 0, False), gathered)
        )

    return lax.fori_loop(0, place, one, state)


def lowpass_taps():
    offsets = np.arange(TAPS) - (TAPS - 1) / 2.0
    window = 0.54 - 0.46 * np.cos(2.0 * np.pi * np.arange(TAPS) / (TAPS - 1))
    angles = np.pi * 0.8 * offsets / DECIM
    values = np.sin(angles) / angles * window
    return values / values.sum()


def filter_tables():
    tap_values = lowpass_taps()
    carried = TAPS - DECIM
    outputs = np.arange(WIN)[:, None]
    inputs = np.arange(DECIM * WIN)[None, :]
    lag_main = DECIM * outputs + DECIM - 1 - inputs
    main_table = np.where(
        (lag_main >= 0) & (lag_main < TAPS), tap_values[np.clip(lag_main, 0, TAPS - 1)], 0.0
    )
    earlier_ids = np.arange(carried)[None, :]
    lag_edge = DECIM * outputs + DECIM - 1 - (earlier_ids - carried)
    edge_table = np.where(
        (lag_edge >= 0) & (lag_edge < TAPS), tap_values[np.clip(lag_edge, 0, TAPS - 1)], 0.0
    )
    return (jnp.asarray(main_table, jnp.bfloat16), jnp.asarray(edge_table, jnp.bfloat16))


def running_tables():
    forget = math.exp(-1.0 / WIN)
    step_ids = np.arange(WIN)
    step_gaps = step_ids[:, None] - step_ids[None, :]
    within = np.where(step_gaps >= 0, (1.0 - forget) * forget ** np.maximum(step_gaps, 0), 0.0)
    window_ids = np.arange(NW)
    lag_table = np.arange(NW + 1)[:, None] - 1 - window_ids[None, :]
    carry_table = np.where(lag_table >= 0, forget ** (WIN * np.maximum(lag_table, 0)), 0.0)
    window_powers = forget ** (WIN * window_ids)
    rising = forget ** (step_ids + 1.0)
    return (
        jnp.asarray(within, jnp.float32),
        jnp.asarray(carry_table, jnp.float32),
        jnp.asarray(window_powers, jnp.float32),
        jnp.asarray(rising, jnp.float32),
    )


def spectrum_table():
    time_ids = np.arange(WIN)
    freq_ids = np.arange(1, NB + 1)
    phases = 2.0 * np.pi * freq_ids[:, None] * time_ids[None, :] / WIN
    return jnp.asarray(
        np.concatenate([np.cos(phases), -np.sin(phases)], axis=0) / np.sqrt(WIN), jnp.bfloat16
    )


def gather_groups(whitened):
    return lax.all_gather(whitened[None], "tm", axis=0, tiled=True)


def body(raw_strain, source_blocks, band_bins):
    channels_here = raw_strain.shape[1]
    carried = TAPS - DECIM
    raw_window = DECIM * WIN
    windows = raw_strain.reshape(NW, raw_window, channels_here)
    main_table, edge_table = filter_tables()
    previous = from_behind(raw_strain[NW * raw_window - carried :], "tm", 1)
    earlier = jnp.concatenate([previous[None], windows[: NW - 1, raw_window - carried :]], axis=0)
    decimated = jnp.einsum("mr,wrc->wmc", main_table, windows, preferred_element_type=jnp.float32)
    decimated = decimated + jnp.einsum(
        "mq,wqc->wmc", edge_table, earlier, preferred_element_type=jnp.float32
    )
    within, carry_table, window_powers, rising = running_tables()
    energy = decimated * decimated
    local_run = jnp.einsum("tu,wuc->wtc", within, energy, precision=lax.Precision.HIGHEST)
    window_ends = local_run[:, WIN - 1, :]
    entering = jnp.dot(carry_table, window_ends, precision=lax.Precision.HIGHEST)
    block_total = entering[NW]

    def compose(earlier_map, later_map):
        return (earlier_map[0] * later_map[0], later_map[0] * earlier_map[1] + later_map[1])

    factors = jnp.full((channels_here,), math.exp(-NW), jnp.float32)
    prefix_maps = carried_in(
        (factors, block_total), "tm", compose, (jnp.ones_like(factors), jnp.zeros_like(block_total))
    )
    incoming = prefix_maps[1]
    starts = entering[:NW] + window_powers[:, None] * incoming[None, :]
    running = local_run + rising[None, :, None] * starts[:, None, :]
    normalized = (decimated / jnp.sqrt(jnp.maximum(running, 0.01))).astype(jnp.bfloat16)
    spectra = jnp.einsum(
        "kt,wtc->wkc", spectrum_table(), normalized, preferred_element_type=jnp.float32
    )
    band_power = jnp.sum(spectra * spectra, axis=1) / NB
    bin_index = jnp.arange(NB)
    band_keep = ((bin_index >= band_bins[0]) & (bin_index < band_bins[1])).astype(jnp.float32)
    band_keep = jnp.concatenate([band_keep, band_keep])
    whitened = (
        spectra * band_keep[None, :, None] / jnp.sqrt(jnp.maximum(band_power, 0.1))[:, None, :]
    ).astype(jnp.bfloat16)
    groups = lax.axis_size("tm")
    src_share = 2 * VS // groups
    own_all = gather_groups(whitened)
    gathered = lax.all_gather(whitened, "chan", axis=2, tiled=True)
    first_block = lax.dynamic_slice_in_dim(gathered, source_blocks[0] * channels_here, VS, 2)
    second_block = lax.dynamic_slice_in_dim(gathered, source_blocks[1] * channels_here, VS, 2)
    picked = jnp.concatenate([first_block, second_block], axis=2)
    shares = lax.all_to_all(picked[None], "tm", split_axis=3, concat_axis=0, tiled=True)
    own_spectra = own_all.reshape(groups, NW, 2, NB, channels_here)
    source_groups = shares.reshape(groups, NW, 2, NB, src_share)
    rotated = jnp.stack([-source_groups[:, :, 1], source_groups[:, :, 0]], axis=2)
    turned = jnp.stack([source_groups, rotated], axis=3)
    stack_scale = 1.0 / math.sqrt(groups * NW)

    def add_group(group_index, stacked_sum):
        own_block = lax.dynamic_index_in_dim(own_spectra, group_index, 0, False)
        src_block = lax.dynamic_index_in_dim(turned, group_index, 0, False)
        group_term = (
            jnp.einsum("wpkc,wpqks->sqkc", own_block, src_block, preferred_element_type=jnp.float32)
            * stack_scale
        )
        return stacked_sum + lax.optimization_barrier(group_term.astype(jnp.bfloat16)).astype(
            jnp.float32
        )

    stacked_sum = lax.fori_loop(
        0, groups, add_group, jnp.zeros((src_share, 2, NB, channels_here), jnp.float32)
    )
    return stacked_sum.astype(jnp.bfloat16)


def solution(mesh):
    in_specs = (P("tm", "chan"), P(), P())
    out_specs = P("tm", None, None, "chan")
    return jax.shard_map(body, mesh=mesh, in_specs=in_specs, out_specs=out_specs, check_vma=False)
```

profile of v0, /device:TPU:1, one launch (start us, length us, event | category | flops | bytes accessed | tf_op | source)
XLA Modules:
  0.0 365.0 jit_solution(10536839834026932320)
XLA Ops:
  7.4 0.7 slice.33
  8.1 4.9 %collective-permute-start = (bf16[60,128]{1,0:T(8,128)(2,1)S(1)}, bf16[60,128]{1,0:T(8,128)(2,1)S(1)}, u32[]{:S(2)}, u32[]{:S(2)}) collective-permute-start(bf16[60,128]{1,0:T(8,128)(2,1)S(1)} %slice.33), channel_id=1, source_target_pairs={{0,32},{32,64},{64,96},{96,128},{128,160},{160,192},{192,224},{1,3... | collective-permute-start | bytes 46088 | tf_op jit(solution)/shard_map/ppermute | solution.py:19
  13.0 1.3 fusion.14
  14.4 10.4 %fusion.15 = f32[500,16,128]{2,0,1:T(8,128)} fusion(bf16[500,2000,1]{0,1,2:T(8,128)(2,1)} %constant.102, bf16[16,2000,128]{2,1,0:T(8,128)(2,1)} %bitcast.88), kind=kOutput, calls=%fused_computation.37 | convolution fusion | flops 4096000000 | bytes 14288000 | tf_op jit(solution)/shard_map/mr,wrc->wmc/dot_general | solution.py:99
  24.8 1.3 compare_and_fusion
  26.1 1.0 slice.44
  27.2 3.0 bitcast_add_fusion.1
  30.3 7.4 %fusion.4 = f32[16,500,128]{2,1,0:T(8,128)S(1)} fusion(f32[500,500,1]{1,0,2:T(8,128)S(1)} %copy-done.2, f32[16,128,500]{1,2,0:T(8,128)S(1)} %bitcast_add_fusion.1), kind=kOutput, calls=%fused_computation.16 | convolution fusion | flops 6145024000 | bytes 9192000 | tf_op jit(solution)/shard_map/tu,wuc->wtc/dot_general | solution.py:105
  37.7 1.9 copy-done.1
  39.7 0.1 fusion.16
  39.8 11.2 %all-gather.1 = f32[8,1,128]{2,1,0:T(1,128)S(1)} all-gather(f32[1,1,128]{2,1,0:T(1,128)S(1)} %slice_bitcast_fusion), channel_id=1, replica_groups=mesh['tm'=8,'chan'=32] {'tm'}, dimensions={0}, use_global_device_ids=true | all-gather | bytes 4608 | tf_op jit(solution)/shard_map/all_gather | solution.py:24
  51.1 0.2 while.27
  51.4 4.4 %multiply_reduce_fusion = (f32[16,128]{1,0:T(8,128)S(1)}, f32[16,128,40]{1,2,0:T(8,128)S(1)}) fusion(bf16[40,500,1]{1,0,2:T(8,128)(2,1)S(1)} %copy-done.4, f32[16,128,500]{1,2,0:T(8,128)} %copy-done, f32[16,500,128]{2,1,0:T(8,128)} %copy-done.1, f32[16,128]{1,0:T(8,128)S(1)} %slice_add_fusion, f32[500]{0:T(512)S(1)} %copy-done.7), kind=kOutput, calls=%fused_computation.21 | convolution fusion | flops 87201792 | bytes 8578064 | tf_op jit(solution)/shard_map/kt,wtc->wkc/dot_general | solution.py:121
  55.8 0.8 fusion.10
  56.6 0.6 fusion.13
  58.5 149.2 %all-gather.5.cloned.1.call-done = bf16[16,40,4096]{2,1,0:T(8,128)(2,1)} async-done(((bf16[16,40,128]{2,1,0:T(8,128)(2,1)}), bf16[16,40,4096]{2,1,0:T(8,128)(2,1)}) %all-gather.5.cloned.1.call-update) | async-done | bytes 5242896 | tf_op jit(solution)/shard_map/all_gather | solution.py:134
  207.7 1.5 constant_dynamic-slice_fusion.3
  209.4 5.7 %copy.23 = bf16[1,16,40,1280]{2,1,0,3:T(8,128)(2,1)} copy(bf16[1,16,40,1280]{3,2,1,0:T(8,128)(2,1)S(1)} %maximum_bitcast_fusion.1) | data formatting | bytes 3276800 | tf_op jit(solution)/shard_map/broadcast_in_dim | solution.py:138
  215.1 10.2 %reshape.38 = bf16[8,2,51200]{2,1,0:T(2,128)(2,1)} reshape(bf16[1280,1,16,40]{3,2,1,0:T(8,128)(2,1)} %bitcast.81) | data formatting | bytes 3276800
  225.3 5.8 %all-to-all-start = ((bf16[8,2,51200]{2,1,0:T(2,128)(2,1)}), bf16[8,2,51200]{2,1,0:T(2,128)(2,1)}, u32[]{:S(2)}, u32[]{:S(2)}) async-start(bf16[8,2,51200]{2,1,0:T(2,128)(2,1)} %reshape.38), calls=%async_computation | async-start | bytes 3276800 | tf_op jit(solution)/shard_map/all_to_all | solution.py:138
  231.1 0.6 all-gather.7.cloned.1.call-update
  231.6 50.4 %all-gather.7.cloned.1.call-done = bf16[128,40,128]{2,1,0:T(8,128)(2,1)} async-done(((bf16[16,40,128]{2,1,0:T(8,128)(2,1)}), bf16[128,40,128]{2,1,0:T(8,128)(2,1)}) %all-gather.7.cloned.1.call-update) | async-done | bytes 1310736 | tf_op jit(solution)/shard_map/all_gather | solution.py:88
  282.0 2.8 copy.27
  284.8 10.4 %reshape.39 = bf16[1280,1,16,40]{3,2,1,0:T(8,128)(2,1)} reshape(bf16[8,2,51200]{2,1,0:T(2,128)(2,1)} %all-to-all-done) | data formatting | bytes 3276800
  295.2 8.5 %copy.33 = bf16[1,16,40,8,160]{4,3,2,1,0:T(8,128)(2,1)} copy(bf16[1,16,40,8,160]{2,1,4,3,0:T(8,128)(2,1)} %bitcast.82) | data formatting | bytes 3276800 | tf_op jit(solution)/shard_map/all_to_all | solution.py:138
  303.7 3.2 copy.25
  307.0 0.2 slice_negate_fusion
  307.1 0.4 maximum_bitcast_fusion
  307.6 3.3 pad_maximum_fusion
  310.9 43.9 %while.28 = (s32[]{:T(128)}, f32[160,2,20,128]{3,0,1,2:T(8,128)S(1)}, bf16[8,16,2,2,20,160]{5,1,4,2,0,3:T(8,128)(2,1)}, bf16[8,16,2,20,128]{4,1,0,3,2:T(8,128)(2,1)}, s32[]{:T(128)}, /*index=5*/s32[]{:T(128)}) while((s32[]{:T(128)}, f32[160,2,20,128]{3,0,1,2:T(8,128)S(1)}, bf16[8,16,2,2,20,160]{5,1,4,2,0,3:T(8,128)(2,1)}, ...), condition=%wide.region_4.5_spmd.clone, body=%wide.region_3.4_spmd.clone.sunk | while | flops 56524800 | bytes 10650703 | solution.py:156
  310.9 3.0 fusion.25
  313.9 2.5 select_add_fusion.2
  316.4 3.0 fusion.25
  319.4 2.5 select_add_fusion.2
  321.9 3.0 fusion.25
  324.9 2.5 select_add_fusion.2
  327.4 3.0 fusion.25
  330.4 2.5 select_add_fusion.2
  332.9 3.0 fusion.25
  335.9 2.5 select_add_fusion.2
  338.4 3.0 fusion.25
  341.3 2.5 select_add_fusion.2
  343.9 3.0 fusion.25
  346.8 2.5 select_add_fusion.2
  349.4 3.0 fusion.25
  352.3 2.5 select_add_fusion.2
  354.8 0.3 convert_element_type.33
  355.1 2.4 copy.30
  (31 shorter events, 0.4 us)
Async XLA Ops:
  7.4 200.3 %all-gather.5.cloned.1.call-start = ((), (), s32[]{:S(2)}) async-start(), calls=%async_computation.1 | async-start | bytes 5406720 | tf_op jit(solution)/shard_map/all_gather | solution.py:134
  8.1 19.1 %collective-permute-start = (bf16[60,128]{1,0:T(8,128)(2,1)S(1)}, bf16[60,128]{1,0:T(8,128)(2,1)S(1)}, u32[]{:S(2)}, u32[]{:S(2)}) collective-permute-start(bf16[60,128]{1,0:T(8,128)(2,1)S(1)} %slice.33), channel_id=1, source_target_pairs={{0,32},{32,64},{64,96},{96,128},{128,160},{160,192},{192,224},{1,3... | collective-permute-start | bytes 46088 | tf_op jit(solution)/shard_map/ppermute | solution.py:19
  14.4 12.8 %copy-start.3 = (bf16[500,60,1]{0,1,2:T(8,128)(2,1)S(1)}, bf16[500,60,1]{0,1,2:T(8,128)(2,1)}, u32[]{:S(2)}) copy-start(bf16[500,60,1]{0,1,2:T(8,128)(2,1)} %constant.103) | copy-start | bytes 180004
  27.2 3.0 copy-start.2
  30.2 7.5 %copy-start = (f32[16,128,500]{1,2,0:T(8,128)}, f32[16,128,500]{1,2,0:T(8,128)S(1)}, u32[]{:S(2)}) copy-start(f32[16,128,500]{1,2,0:T(8,128)S(1)} %bitcast_add_fusion.1) | copy-start | bytes 12288004
  30.2 9.4 %copy-start.5 = (f32[17,16]{1,0:T(8,128)S(1)}, f32[17,16]{1,0:T(8,128)}, u32[]{:S(2)}) copy-start(f32[17,16]{1,0:T(8,128)} %constant.98.clone) | copy-start | bytes 3268
  30.2 21.0 %copy-start.8 = (f32[16]{0:T(128)S(1)}, f32[16]{0:T(128)}, u32[]{:S(2)}) copy-start(f32[16]{0:T(128)} %constant.99.clone) | copy-start | bytes 196
  30.2 21.1 %copy-start.4 = (bf16[40,500,1]{1,0,2:T(8,128)(2,1)S(1)}, bf16[40,500,1]{1,0,2:T(8,128)(2,1)}, u32[]{:S(2)}) copy-start(bf16[40,500,1]{1,0,2:T(8,128)(2,1)} %constant.105) | copy-start | bytes 120004
  30.3 21.1 %copy-start.7 = (f32[500]{0:T(512)S(1)}, f32[500]{0:T(512)}, u32[]{:S(2)}) copy-start(f32[500]{0:T(512)} %constant.100.clone) | copy-start | bytes 6004
  37.7 2.0 copy-start.1
  51.4 5.3 %copy-start.6 = (s32[2]{0:T(128)S(1)}, s32[2]{0:T(128)}, u32[]{:S(2)}) copy-start(s32[2]{0:T(128)} %param.15) | copy-start | bytes 28
  225.3 59.5 %all-to-all-start = ((bf16[8,2,51200]{2,1,0:T(2,128)(2,1)}), bf16[8,2,51200]{2,1,0:T(2,128)(2,1)}, u32[]{:S(2)}, u32[]{:S(2)}) async-start(bf16[8,2,51200]{2,1,0:T(2,128)(2,1)} %reshape.38), calls=%async_computation | async-start | bytes 3276800 | tf_op jit(solution)/shard_map/all_to_all | solution.py:138
  231.1 51.0 %all-gather.7.cloned.1.call-start = ((), (), s32[]{:S(2)}) async-start(), calls=%async_computation.2 | async-start | bytes 1474560 | tf_op jit(solution)/shard_map/all_gather | solution.py:88
Sparse Core Ops, SparseCore 0:
  56.7 150.9 all-gather.4
Sparse Core Ops, SparseCore 1:
  233.3 48.7 all-gather.6
where the time goes:
time: 366 us; the launch traced here: 365 us
  waiting for transfers between devices  200 us (55%)
  local copies, waits for them, and re-layouts  50.5 us (14%)
  matrix products  49.2 us (13%)
  other arithmetic  26.5 us (7%)
  between operations  16.4 us (4%)
  blocking collectives  11.2 us (3%)
  starting transfers between devices  10.7 us (3%)
    all_gather x1, waiting for transfers between devices, body(): gathered = lax.all_gather(whitened, 'chan', axis=2, tiled=True)  149 us
    all_gather x1, waiting for transfers between devices, gather_groups(): return lax.all_gather(whitened[None], 'tm', axis=0, tiled=True)  50.4 us
    dot_general x8, matrix products, add_group(): jnp.einsum('wpkc,wpqks->sqkc', own_block, src_block, preferred_element_ty...  23.8 us
    unnamed x21, local copies, waits for them, and re-layouts  22.6 us
    add x8, other arithmetic, add_group(): stacked_sum + lax.optimization_barrier(group_term.astype(jnp.bfloat16)).a...  20 us
    all_to_all x2, local copies, waits for them, and re-layouts, body(): lax.all_to_all(picked[None], 'tm', split_axis=3, concat_axis=0, tiled=True)  11.7 us
    all_gather x1, blocking collectives, carried_in(): gathered = jax.tree.map(lambda a: lax.all_gather(a, axis), part)  11.2 us
    dot_general x1, matrix products, body(): jnp.einsum('mr,wrc->wmc', main_table, windows, preferred_element_type=jnp...  10.4 us
  transfers between devices with their start and end apart: 4, of which 2 were waited for; matrix products, arithmetic and copies ran while one was open for 5% of the time, Pallas kernels for 0%

commit v1 on v0

--- a/solution.py
+++ b/solution.py
@@ -135,7 +135,11 @@
     first_block = lax.dynamic_slice_in_dim(gathered, source_blocks[0] * channels_here, VS, 2)
     second_block = lax.dynamic_slice_in_dim(gathered, source_blocks[1] * channels_here, VS, 2)
     picked = jnp.concatenate([first_block, second_block], axis=2)
-    shares = lax.all_to_all(picked[None], "tm", split_axis=3, concat_axis=0, tiled=True)
+    block = picked[None]
+    n_dev = lax.axis_size("tm")
+    parts = jnp.stack(jnp.split(block, n_dev, axis=3), axis=0)
+    parts = lax.all_to_all(parts, "tm", split_axis=0, concat_axis=0)
+    shares = jnp.concatenate(parts, axis=0)
     own_spectra = own_all.reshape(groups, NW, 2, NB, channels_here)
     source_groups = shares.reshape(groups, NW, 2, NB, src_share)
     rotated = jnp.stack([-source_groups[:, :, 1], source_groups[:, :, 0]], axis=2)

time: 366 us -> 355 us (0.970)
  local copies, waits for them, and re-layouts: 50.5 us -> 21.5 us
  waiting for transfers between devices: 200 us -> 218 us
    all_to_all x1, waiting for transfers between devices: 0.01 us -> 18.3 us  [body(): parts = lax.all_to_all(parts, 'tm', split_axis=0, concat_axis=0)]
    unnamed x21 -> x26, local copies, waits for them, and re-layouts: 22.6 us -> 7.96 us
    all_to_all x2 -> x1, local copies, waits for them, and re-layouts: 11.7 us -> 2.3 us  [body(): parts = lax.all_to_all(parts, 'tm', split_axis=0, concat_axis=0)]
    broadcast_in_dim x1 -> x0, local copies, waits for them, and re-layouts: 5.72 us -> none  [body(): picked[None]]
  transfers between devices with their start and end apart: 4 -> 4, of which waited for: 2 -> 3; matrix products, arithmetic and copies ran while one was open for 5% -> 5% of each run, Pallas kernels for 0% -> 0%
where the time goes in v1:
time: 355 us; the launch traced here: 354 us
  waiting for transfers between devices  218 us (61%)
  matrix products  49.2 us (14%)
  other arithmetic  26.5 us (7%)
  local copies, waits for them, and re-layouts  21.5 us (6%)
  between operations  16.3 us (5%)
  blocking collectives  11.2 us (3%)
  starting transfers between devices  10.8 us (3%)
    all_gather x1, waiting for transfers between devices, body(): gathered = lax.all_gather(whitened, 'chan', axis=2, tiled=True)  149 us
    all_gather x1, waiting for transfers between devices, gather_groups(): return lax.all_gather(whitened[None], 'tm', axis=0, tiled=True)  50.3 us
    dot_general x8, matrix products, add_group(): jnp.einsum('wpkc,wpqks->sqkc', own_block, src_block, preferred_element_ty...  23.8 us
    add x8, other arithmetic, add_group(): stacked_sum + lax.optimization_barrier(group_term.astype(jnp.bfloat16)).a...  20 us
    all_to_all x1, waiting for transfers between devices, body(): parts = lax.all_to_all(parts, 'tm', split_axis=0, concat_axis=0)  18.3 us
    all_gather x1, blocking collectives, carried_in(): gathered = jax.tree.map(lambda a: lax.all_gather(a, axis), part)  11.2 us
    dot_general x1, matrix products, body(): jnp.einsum('mr,wrc->wmc', main_table, windows, preferred_element_type=jnp...  10.4 us
    unnamed x26, local copies, waits for them, and re-layouts  7.96 us
  transfers between devices with their start and end apart: 4, of which 3 were waited for; matrix products, arithmetic and copies ran while one was open for 5% of the time, Pallas kernels for 0%

profile of v1, /device:TPU:1, one launch (start us, length us, event | category | flops | bytes accessed | tf_op | source)
XLA Modules:
  0.0 354.3 jit_solution(15364803383288666050)
XLA Ops:
  7.4 0.7 slice.33
  8.1 4.9 %collective-permute-start = (bf16[60,128]{1,0:T(8,128)(2,1)S(1)}, bf16[60,128]{1,0:T(8,128)(2,1)S(1)}, u32[]{:S(2)}, u32[]{:S(2)}) collective-permute-start(bf16[60,128]{1,0:T(8,128)(2,1)S(1)} %slice.33), channel_id=1, source_target_pairs={{0,32},{32,64},{64,96},{96,128},{128,160},{160,192},{192,224},{1,3... | collective-permute-start | bytes 46088 | tf_op jit(solution)/shard_map/ppermute | solution.py:19
  13.0 1.3 fusion.22
  14.4 10.4 %fusion.23 = f32[500,16,128]{2,0,1:T(8,128)} fusion(bf16[500,2000,1]{0,1,2:T(8,128)(2,1)} %constant.102, bf16[16,2000,128]{2,1,0:T(8,128)(2,1)} %bitcast.113), kind=kOutput, calls=%fused_computation.53 | convolution fusion | flops 4096000000 | bytes 14288000 | tf_op jit(solution)/shard_map/mr,wrc->wmc/dot_general | solution.py:99
  24.8 1.3 compare_and_fusion
  26.1 1.0 slice.44
  27.2 3.0 bitcast_add_fusion.1
  30.3 7.4 %fusion.4 = f32[16,500,128]{2,1,0:T(8,128)S(1)} fusion(f32[500,500,1]{1,0,2:T(8,128)S(1)} %copy-done.2, f32[16,128,500]{1,2,0:T(8,128)S(1)} %bitcast_add_fusion.1), kind=kOutput, calls=%fused_computation.16 | convolution fusion | flops 6145024000 | bytes 9192000 | tf_op jit(solution)/shard_map/tu,wuc->wtc/dot_general | solution.py:105
  37.7 1.9 copy-done.1
  39.8 11.2 %all-gather.1 = f32[8,1,128]{2,1,0:T(1,128)S(1)} all-gather(f32[1,1,128]{2,1,0:T(1,128)S(1)} %slice_bitcast_fusion.8), channel_id=1, replica_groups=mesh['tm'=8,'chan'=32] {'tm'}, dimensions={0}, use_global_device_ids=true | all-gather | bytes 4608 | tf_op jit(solution)/shard_map/all_gather | solution.py:24
  51.4 4.4 %multiply_reduce_fusion = (f32[16,128]{1,0:T(8,128)S(1)}, f32[16,128,40]{1,2,0:T(8,128)S(1)}) fusion(bf16[40,500,1]{1,0,2:T(8,128)(2,1)S(1)} %copy-done.4, f32[16,128,500]{1,2,0:T(8,128)} %copy-done, f32[16,500,128]{2,1,0:T(8,128)} %copy-done.1, f32[16,128]{1,0:T(8,128)S(1)} %slice_add_fusion, f32[500]{0:T(512)S(1)} %copy-done.7), kind=kOutput, calls=%fused_computation.37 | convolution fusion | flops 87201792 | bytes 8578064 | tf_op jit(solution)/shard_map/kt,wtc->wkc/dot_general | solution.py:121
  55.8 0.8 fusion.18
  56.6 0.6 fusion.21
  58.4 149.3 %all-gather.5.cloned.1.call-done = bf16[16,40,4096]{2,1,0:T(8,128)(2,1)} async-done(((bf16[16,40,128]{2,1,0:T(8,128)(2,1)}), bf16[16,40,4096]{2,1,0:T(8,128)(2,1)}) %all-gather.5.cloned.1.call-update) | async-done | bytes 5242896 | tf_op jit(solution)/shard_map/all_gather | solution.py:134
  207.7 1.5 constant_dynamic-slice_fusion.3
  209.4 0.8 fusion.14
  210.1 0.9 fusion.13
  211.0 0.9 fusion.12
  211.9 0.9 fusion.11
  212.8 0.7 fusion.10
  213.6 0.9 fusion.9
  214.5 0.9 fusion.8
  215.4 0.9 fusion.7
  216.3 5.8 %all-to-all-start = ((bf16[8,1,16,40,160]{4,3,2,1,0:T(8,128)(2,1)}), bf16[8,1,16,40,160]{4,3,2,1,0:T(8,128)(2,1)}, u32[]{:S(2)}, u32[]{:S(2)}) async-start(bf16[8,1,16,40,160]{4,3,2,1,0:T(8,128)(2,1)} %fusion.7), calls=%async_computation | async-start | bytes 5242880 | tf_op jit(solution)/shard_map/all_to_all | solution.py:141
  222.1 0.6 all-gather.7.cloned.1.call-update
  222.7 50.3 %all-gather.7.cloned.1.call-done = bf16[128,40,128]{2,1,0:T(8,128)(2,1)} async-done(((bf16[16,40,128]{2,1,0:T(8,128)(2,1)}), bf16[128,40,128]{2,1,0:T(8,128)(2,1)}) %all-gather.7.cloned.1.call-update) | async-done | bytes 1310736 | tf_op jit(solution)/shard_map/all_gather | solution.py:88
  272.9 2.7 copy.24
  275.6 18.3 %all-to-all-done = bf16[8,1,16,40,160]{4,3,2,1,0:T(8,128)(2,1)} async-done(((bf16[8,1,16,40,160]{4,3,2,1,0:T(8,128)(2,1)}), bf16[8,1,16,40,160]{4,3,2,1,0:T(8,128)(2,1)}, u32[]{:S(2)}, u32[]{:S(2)}) %all-to-all-start) | async-done | bytes 1638432 | tf_op jit(solution)/shard_map/all_to_all | solution.py:141
  293.9 2.3 copy.22
  296.9 3.3 pad_maximum_fusion
  300.2 43.9 %while.28 = (s32[]{:T(128)}, f32[160,2,20,128]{3,0,1,2:T(8,128)S(1)}, bf16[8,16,2,2,20,160]{5,1,4,2,0,3:T(8,128)(2,1)}, bf16[8,16,2,20,128]{4,1,0,3,2:T(8,128)(2,1)}, s32[]{:T(128)}, /*index=5*/s32[]{:T(128)}) while((s32[]{:T(128)}, f32[160,2,20,128]{3,0,1,2:T(8,128)S(1)}, bf16[8,16,2,2,20,160]{5,1,4,2,0,3:T(8,128)(2,1)}, ...), condition=%wide.region_4.5_spmd.clone, body=%wide.region_3.4_spmd.clone.sunk | while | flops 56524800 | bytes 10650703 | solution.py:160
  300.2 3.0 fusion.33
  303.2 2.5 select_add_fusion.2
  305.7 3.0 fusion.33
  308.7 2.5 select_add_fusion.2
  311.2 3.0 fusion.33
  314.2 2.5 select_add_fusion.2
  316.7 3.0 fusion.33
  319.7 2.5 select_add_fusion.2
  322.2 3.0 fusion.33
  325.1 2.5 select_add_fusion.2
  327.7 3.0 fusion.33
  330.6 2.5 select_add_fusion.2
  333.2 3.0 fusion.33
  336.1 2.5 select_add_fusion.2
  338.6 3.0 fusion.33
  341.6 2.5 select_add_fusion.2
  344.4 2.4 copy.27
  (35 shorter events, 1.6 us)
Async XLA Ops:
  7.4 200.3 %all-gather.5.cloned.1.call-start = ((), (), s32[]{:S(2)}) async-start(), calls=%async_computation.1 | async-start | bytes 5406720 | tf_op jit(solution)/shard_map/all_gather | solution.py:134
  8.1 19.1 %collective-permute-start = (bf16[60,128]{1,0:T(8,128)(2,1)S(1)}, bf16[60,128]{1,0:T(8,128)(2,1)S(1)}, u32[]{:S(2)}, u32[]{:S(2)}) collective-permute-start(bf16[60,128]{1,0:T(8,128)(2,1)S(1)} %slice.33), channel_id=1, source_target_pairs={{0,32},{32,64},{64,96},{96,128},{128,160},{160,192},{192,224},{1,3... | collective-permute-start | bytes 46088 | tf_op jit(solution)/shard_map/ppermute | solution.py:19
  14.4 12.8 %copy-start.3 = (bf16[500,60,1]{0,1,2:T(8,128)(2,1)S(1)}, bf16[500,60,1]{0,1,2:T(8,128)(2,1)}, u32[]{:S(2)}) copy-start(bf16[500,60,1]{0,1,2:T(8,128)(2,1)} %constant.103) | copy-start | bytes 180004
  27.2 3.0 copy-start.2
  30.2 7.5 %copy-start = (f32[16,128,500]{1,2,0:T(8,128)}, f32[16,128,500]{1,2,0:T(8,128)S(1)}, u32[]{:S(2)}) copy-start(f32[16,128,500]{1,2,0:T(8,128)S(1)} %bitcast_add_fusion.1) | copy-start | bytes 12288004
  30.2 9.4 %copy-start.5 = (f32[17,16]{1,0:T(8,128)S(1)}, f32[17,16]{1,0:T(8,128)}, u32[]{:S(2)}) copy-start(f32[17,16]{1,0:T(8,128)} %constant.98.clone) | copy-start | bytes 3268
  30.2 21.0 %copy-start.8 = (f32[16]{0:T(128)S(1)}, f32[16]{0:T(128)}, u32[]{:S(2)}) copy-start(f32[16]{0:T(128)} %constant.99.clone) | copy-start | bytes 196
  30.2 21.1 %copy-start.4 = (bf16[40,500,1]{1,0,2:T(8,128)(2,1)S(1)}, bf16[40,500,1]{1,0,2:T(8,128)(2,1)}, u32[]{:S(2)}) copy-start(bf16[40,500,1]{1,0,2:T(8,128)(2,1)} %constant.105) | copy-start | bytes 120004
  30.3 21.1 %copy-start.7 = (f32[500]{0:T(512)S(1)}, f32[500]{0:T(512)}, u32[]{:S(2)}) copy-start(f32[500]{0:T(512)} %constant.100.clone) | copy-start | bytes 6004
  37.7 2.0 copy-start.1
  51.4 5.3 %copy-start.6 = (s32[2]{0:T(128)S(1)}, s32[2]{0:T(128)}, u32[]{:S(2)}) copy-start(s32[2]{0:T(128)} %param.15) | copy-start | bytes 28
  216.3 77.7 %all-to-all-start = ((bf16[8,1,16,40,160]{4,3,2,1,0:T(8,128)(2,1)}), bf16[8,1,16,40,160]{4,3,2,1,0:T(8,128)(2,1)}, u32[]{:S(2)}, u32[]{:S(2)}) async-start(bf16[8,1,16,40,160]{4,3,2,1,0:T(8,128)(2,1)} %fusion.7), calls=%async_computation | async-start | bytes 5242880 | tf_op jit(solution)/shard_map/all_to_all | solution.py:141
  222.1 50.8 %all-gather.7.cloned.1.call-start = ((), (), s32[]{:S(2)}) async-start(), calls=%async_computation.2 | async-start | bytes 1474560 | tf_op jit(solution)/shard_map/all_gather | solution.py:88
Sparse Core Ops, SparseCore 0:
  56.7 150.9 all-gather.4
Sparse Core Ops, SparseCore 1:
  224.3 48.5 all-gather.6
